TPU v7x, 32 devices: a whole 2x2x4 slice. The times are simulated.
32 devices in a mesh: row: 4 (over y, core), col: 8 (over z, x).
Axes of the slice: x: 2, y: 2, z: 4, core: 2. Of those that a mesh axis runs over, the one named last changes fastest.
Arguments:
- inputs: bfloat16 [512, 12288], P('col', 'row'), may hold values from -6 to 6
- grad_out: bfloat16 [512, 12288], P('col', 'row'), may hold values from -6 to 6
- w_in: bfloat16 [12288, 24576], P('row', 'col'), may hold values from -0.0546875 to 0.0546875
- w_out: bfloat16 [24576, 12288], P('col', 'row'), may hold values from -0.0390625 to 0.0390625
Outputs:
- outputs: bfloat16 [512, 12288], P('col', 'row')
- grad_in: bfloat16 [512, 12288], P('col', 'row')
- grad_w_in: bfloat16 [12288, 24576], P('row', 'col')
- grad_w_out: bfloat16 [24576, 12288], P('col', 'row')
All inputs are finite; a program needn't handle non-finite values.
Results may differ from a plain program's by a relative error of at most 0.019.
Values may be sent and summed in bfloat16 or wider, within the bound.
A program may use at most 192 MiB of HBM per device.

v0:
```python
from functools import partial
import jax
import jax.numpy as jnp
from jax import lax
from jax.sharding import PartitionSpec as P


def col_panel(values):
    return lax.all_gather(values, "col", axis=0, tiled=True)


def contract(left, right, dims):
    return lax.dot_general(
        left, right, ((dims[0], dims[1]), ((), ())), preferred_element_type=jnp.float32
    )


def row_sums(left, right, dims):
    return lax.psum_scatter(
        contract(left, right, dims).astype(jnp.bfloat16), "row", scatter_dimension=0, tiled=True
    ).astype(jnp.float32)


def row_spread(values):
    return lax.all_gather(values, "row", axis=0, tiled=True)


def col_sums(left, right, dims):
    return lax.psum_scatter(
        contract(
            lax.dynamic_slice_in_dim(
                left, jnp.int32(0), left.shape[0] // lax.axis_size("col") * lax.axis_size("col"), 0
            ),
            right,
            dims,
        ).astype(jnp.bfloat16),
        "col",
        scatter_dimension=0,
        tiled=True,
    ).astype(jnp.float32)


def local(inputs, grad_out, w_in, w_out):
    gelu_tanh = partial(jax.nn.gelu, approximate=True)
    input_all = col_panel(inputs)
    cotan_all = None
    hidden_pre = row_sums(input_all, w_in, ((1,), (0,)))
    act_all = row_spread(gelu_tanh(hidden_pre).astype(jnp.bfloat16))
    outputs = col_sums(act_all, w_out, ((1,), (0,))).astype(jnp.bfloat16)
    cotan_all = col_panel(grad_out)
    grad_act = row_sums(cotan_all, w_out, ((1,), (1,)))
    grad_pre = jax.vjp(gelu_tanh, hidden_pre)[1](grad_act)[0].astype(jnp.bfloat16)
    grad_pre_all = row_spread(grad_pre)
    grad_w_out = contract(act_all, cotan_all, ((0,), (0,))).astype(jnp.bfloat16)
    grad_w_in = contract(input_all, grad_pre_all, ((0,), (0,))).astype(jnp.bfloat16)
    grad_in = col_sums(grad_pre_all, w_in, ((1,), (1,))).astype(jnp.bfloat16)
    return (outputs, grad_in, grad_w_in, grad_w_out)


def solution(mesh):
    placed = (P("col", "row"), P("col", "row"), P("row", "col"), P("col", "row"))
    return jax.shard_map(
        local,
        mesh=mesh,
        in_specs=placed,
        out_specs=(P("col", "row"), P("col", "row"), P("row", "col"), P("col", "row")),
        check_vma=False,
    )
```

profile of v0, /device:TPU:0, one launch (start us, length us, event | category | flops | bytes accessed | tf_op | source)
XLA Modules:
  0.0 441.4 jit_solution(10468758725500619523)
XLA Ops:
  7.2 0.0 all-gather.9.cloned.1.call-start
  7.2 0.7 all-gather.9.cloned.1.call-update
  7.9 0.0 all-gather.5.cloned.1.call-start
  7.9 0.7 all-gather.5.cloned.1.call-update
  8.6 0.0 reduce-scatter.9.cloned.1.call-start
  8.7 64.7 %all-gather.9.cloned.1.call-done = bf16[512,3072]{1,0:T(8,128)(2,1)} async-done(((bf16[64,3072]{1,0:T(8,128)(2,1)}), bf16[512,3072]{1,0:T(8,128)(2,1)}) %all-gather.9.cloned.1.call-update) | async-done | bytes 3145744 | tf_op jit(solution)/shard_map/all_gather | solution.py:9
  73.4 15.9 %convolution_convert_fusion.2 = bf16[512,3072]{1,0:T(8,128)(2,1)} fusion(bf16[512,3072]{1,0:T(8,128)(2,1)} %all-gather.9.cloned.1.call-done, bf16[3072,3072]{1,0:T(8,128)(2,1)} %param.7), kind=kOutput, calls=%fused_computation.3 | convolution fusion | flops 9665249280 | bytes 25165824 | tf_op jit(solution)/shard_map/dot_general | solution.py:13
  89.2 0.0 reduce-scatter.9.cloned.1.call-update
  89.3 0.0 reduce-scatter.5.cloned.1.call-start
  89.3 45.4 %all-gather.5.cloned.1.call-done = bf16[512,3072]{1,0:T(8,128)(2,1)} async-done(((bf16[64,3072]{1,0:T(8,128)(2,1)}), bf16[512,3072]{1,0:T(8,128)(2,1)}) %all-gather.5.cloned.1.call-update) | async-done | bytes 3145744 | tf_op jit(solution)/shard_map/all_gather | solution.py:9
  134.7 15.8 %convolution_convert_fusion.4 = bf16[512,3072]{1,0:T(8,128)(2,1)} fusion(bf16[512,3072]{1,0:T(8,128)(2,1)} %all-gather.5.cloned.1.call-done, bf16[3072,3072]{1,0:T(8,128)(2,1)} %param.6), kind=kOutput, calls=%fused_computation.5 | convolution fusion | flops 9665249280 | bytes 25165824 | tf_op jit(solution)/shard_map/dot_general | solution.py:13
  150.4 0.0 reduce-scatter.5.cloned.1.call-update
  150.5 0.0 all-gather.7.cloned.1.call-start
  150.5 23.9 %reduce-scatter.9.cloned.1.call-done = bf16[128,3072]{1,0:T(8,128)(2,1)} async-done(((bf16[512,3072]{1,0:T(8,128)(2,1)}), bf16[128,3072]{1,0:T(8,128)(2,1)}) %reduce-scatter.9.cloned.1.call-update) | async-done | bytes 786448 | tf_op jit(solution)/shard_map/reduce_scatter | solution.py:19
  174.4 41.1 %reduce-scatter.5.cloned.1.call-done = bf16[128,3072]{1,0:T(8,128)(2,1)} async-done(((bf16[512,3072]{1,0:T(8,128)(2,1)}), bf16[128,3072]{1,0:T(8,128)(2,1)}) %reduce-scatter.5.cloned.1.call-update) | async-done | bytes 786448 | tf_op jit(solution)/shard_map/reduce_scatter | solution.py:19
  215.5 3.7 fusion.3
  219.2 0.0 all-gather.7.cloned.1.call-update
  219.3 0.0 all-gather.11.cloned.1.call-start
  219.3 0.5 all-gather.11.cloned.1.call-update
  219.8 0.0 reduce-scatter.7.cloned.1.call-start
  219.9 28.1 %all-gather.7.cloned.1.call-done = bf16[512,3072]{1,0:T(8,128)(2,1)} async-done(((bf16[128,3072]{1,0:T(8,128)(2,1)}), bf16[512,3072]{1,0:T(8,128)(2,1)}) %all-gather.7.cloned.1.call-update) | async-done | bytes 3145744 | tf_op jit(solution)/shard_map/all_gather | solution.py:25
  248.0 15.8 %convolution_convert_fusion.3 = bf16[512,3072]{1,0:T(8,128)(2,1)} fusion(bf16[512,3072]{1,0:T(8,128)(2,1)} %all-gather.7.cloned.1.call-done, bf16[3072,3072]{1,0:T(8,128)(2,1)} %param.7), kind=kOutput, calls=%fused_computation.4 | convolution fusion | flops 9665249280 | bytes 25165824 | tf_op jit(solution)/shard_map/dot_general | solution.py:13
  263.8 0.0 reduce-scatter.7.cloned.1.call-update
  263.8 0.2 reduce-scatter.11.cloned.1.call-start
  264.0 14.5 %all-gather.11.cloned.1.call-done = bf16[512,3072]{1,0:T(8,128)(2,1)} async-done(((bf16[128,3072]{1,0:T(8,128)(2,1)}), bf16[512,3072]{1,0:T(8,128)(2,1)}) %all-gather.11.cloned.1.call-update) | async-done | bytes 3145744 | tf_op jit(solution)/shard_map/all_gather | solution.py:25
  278.5 15.9 %convolution_convert_fusion.1 = bf16[512,3072]{1,0:T(8,128)(2,1)} fusion(bf16[512,3072]{1,0:T(8,128)(2,1)} %all-gather.11.cloned.1.call-done, bf16[3072,3072]{1,0:T(8,128)(2,1)} %param.6), kind=kOutput, calls=%fused_computation.2 | convolution fusion | flops 9665249280 | bytes 25165824 | tf_op jit(solution)/shard_map/dot_general | solution.py:13
  294.5 0.0 copy-start.1
  294.5 0.0 reduce-scatter.11.cloned.1.call-update
  294.5 1.9 copy-done.1
  296.4 15.1 %convert_bitcast_fusion = bf16[3072,3072]{0,1:T(8,128)(2,1)} fusion(bf16[512,3072]{1,0:T(8,128)(2,1)} %all-gather.11.cloned.1.call-done, bf16[512,3072]{1,0:T(8,128)(2,1)S(1)} %copy-done.1), kind=kOutput, calls=%fused_computation | convolution fusion | flops 9673113600 | bytes 25165824 | tf_op jit(solution)/shard_map/dot_general | solution.py:13
  311.5 0.0 copy-start
  311.5 24.8 %copy.8 = bf16[3072,3072]{1,0:T(8,128)(2,1)} copy(bf16[3072,3072]{0,1:T(8,128)(2,1)} %convert_bitcast_fusion) | data formatting | bytes 37748736
  336.3 0.0 copy-done
  336.3 15.0 %convolution_convert_fusion = bf16[3072,3072]{1,0:T(8,128)(2,1)} fusion(bf16[512,3072]{1,0:T(8,128)(2,1)} %all-gather.7.cloned.1.call-done, bf16[512,3072]{1,0:T(8,128)(2,1)S(1)} %copy-done), kind=kOutput, calls=%fused_computation.1 | convolution fusion | flops 9673113600 | bytes 25165824 | tf_op jit(solution)/shard_map/dot_general | solution.py:13
  351.3 5.6 %reduce-scatter.7.cloned.1.call-done = bf16[64,3072]{1,0:T(8,128)(2,1)} async-done(((bf16[512,3072]{1,0:T(8,128)(2,1)}), bf16[64,3072]{1,0:T(8,128)(2,1)}) %reduce-scatter.7.cloned.1.call-update) | async-done | bytes 393232 | tf_op jit(solution)/shard_map/reduce_scatter | solution.py:29
  356.9 77.6 %reduce-scatter.11.cloned.1.call-done = bf16[64,3072]{1,0:T(8,128)(2,1)} async-done(((bf16[512,3072]{1,0:T(8,128)(2,1)}), bf16[64,3072]{1,0:T(8,128)(2,1)}) %reduce-scatter.11.cloned.1.call-update) | async-done | bytes 393232 | tf_op jit(solution)/shard_map/reduce_scatter | solution.py:29
Async XLA Ops:
  7.2 66.2 %all-gather.9.cloned.1.call-start = ((), (), s32[]{:S(2)}) async-start(), calls=%async_computation.8 | async-start | bytes 3538944 | tf_op jit(solution)/shard_map/all_gather | solution.py:9
  7.9 126.8 %all-gather.5.cloned.1.call-start = ((), (), s32[]{:S(2)}) async-start(), calls=%async_computation.4 | async-start | bytes 3538944 | tf_op jit(solution)/shard_map/all_gather | solution.py:9
  8.6 165.7 %reduce-scatter.9.cloned.1.call-start = ((), (), s32[]{:S(2)}) async-start(), calls=%async_computation.9 | async-start | bytes 3932160 | tf_op jit(solution)/shard_map/reduce_scatter | solution.py:19
  89.3 126.2 %reduce-scatter.5.cloned.1.call-start = ((), (), s32[]{:S(2)}) async-start(), calls=%async_computation.5 | async-start | bytes 3932160 | tf_op jit(solution)/shard_map/reduce_scatter | solution.py:19
  150.5 97.5 %all-gather.7.cloned.1.call-start = ((), (), s32[]{:S(2)}) async-start(), calls=%async_computation.6 | async-start | bytes 3932160 | tf_op jit(solution)/shard_map/all_gather | solution.py:25
  219.3 59.3 %all-gather.11.cloned.1.call-start = ((), (), s32[]{:S(2)}) async-start(), calls=%async_computation.10 | async-start | bytes 3932160 | tf_op jit(solution)/shard_map/all_gather | solution.py:25
  219.8 137.1 %reduce-scatter.7.cloned.1.call-start = ((), (), s32[]{:S(2)}) async-start(), calls=%async_computation.7 | async-start | bytes 3538944 | tf_op jit(solution)/shard_map/reduce_scatter | solution.py:29
  263.8 170.7 %reduce-scatter.11.cloned.1.call-start = ((), (), s32[]{:S(2)}) async-start(), calls=%async_computation.11 | async-start | bytes 3538944 | tf_op jit(solution)/shard_map/reduce_scatter | solution.py:29
  294.5 1.9 copy-start.1
  311.5 24.8 %copy-start = (bf16[512,3072]{1,0:T(8,128)(2,1)S(1)}, bf16[512,3072]{1,0:T(8,128)(2,1)}, u32[]{:S(2)}) copy-start(bf16[512,3072]{1,0:T(8,128)(2,1)} %all-gather.9.cloned.1.call-done) | copy-start | bytes 9437188
Sparse Core Ops, SparseCore 0:
  10.2 63.1 all-gather.8
  75.5 59.0 all-gather.4
  137.8 36.5 reduce-scatter.8
  177.5 37.9 reduce-scatter.4
  219.4 28.5 all-gather.6
  249.9 28.5 all-gather.10
  282.7 74.2 reduce-scatter.6
  361.1 73.3 reduce-scatter.10
where the time goes:
time: 442 us; the launch traced here: 441 us
  waiting for transfers between devices  303 us (69%)
  matrix products  93.5 us (21%)
  local copies, waits for them, and re-layouts  26.7 us (6%)
  between operations  14.1 us (3%)
    all_gather x2, waiting for transfers between devices, col_panel(): return lax.all_gather(values, 'col', axis=0, tiled=True)  110 us
    dot_general x6, matrix products, contract(): lax.dot_general(left, right, ((dims[0], dims[1]), ((), ())), preferred_el...  93.5 us
    reduce_scatter x2, waiting for transfers between devices, col_sums(): lax.psum_scatter(contract(lax.dynamic_slice_in_dim(left, jnp.int32(0), le...  83.2 us
    reduce_scatter x2, waiting for transfers between devices, row_sums(): lax.psum_scatter(contract(left, right, dims).astype(jnp.bfloat16), 'row',...  65 us
    all_gather x2, waiting for transfers between devices, row_spread(): return lax.all_gather(values, 'row', axis=0, tiled=True)  42.5 us
    unnamed x5, local copies, waits for them, and re-layouts  26.7 us
  transfers between devices with their start and end apart: 8, of which 8 were waited for; matrix products, arithmetic and copies ran while one was open for 27% of the time, Pallas kernels for 0%

commit v1 on v0

--- a/solution.py
+++ b/solution.py
@@ -3,6 +3,19 @@
 import jax.numpy as jnp
 from jax import lax
 from jax.sharding import PartitionSpec as P
+
+
+def gather_around(x, axis, dim):
+    length, index, rows = (lax.axis_size(axis), lax.axis_index(axis), x.shape[dim])
+    right = [(i, (i + 1) % length) for i in range(length)]
+    out = jnp.zeros((*x.shape[:dim], length * rows, *x.shape[dim + 1 :]), x.dtype)
+    held = x
+    for lap in range(length):
+        owner = (index - lap) % length
+        out = lax.dynamic_update_slice_in_dim(out, held, owner * rows, axis=dim)
+        if lap < length - 1:
+            held = lax.ppermute(held, axis, right)
+    return out
 
 
 def col_panel(values):
@@ -22,7 +35,7 @@
 
 
 def row_spread(values):
-    return lax.all_gather(values, "row", axis=0, tiled=True)
+    return gather_around(values, "row", 0)
 
 
 def col_sums(left, right, dims):

time: 442 us -> 412 us (0.932)
  waiting for transfers between devices: 303 us -> 265 us
  local copies, waits for them, and re-layouts: 26.7 us -> 31.8 us
  starting transfers between devices: 0.5 us -> 4.93 us
    ppermute x0 -> x6, waiting for transfers between devices: none -> 59.6 us  [gather_around(): held = lax.ppermute(held, axis, right)]
    all_gather x2 -> x0, waiting for transfers between devices: 42.5 us -> none  [row_spread(): return lax.all_gather(values, 'row', axis=0, tiled=True)]
    reduce_scatter x2, waiting for transfers between devices: 83.2 us -> 41.5 us  [col_sums(): lax.psum_scatter(contract(lax.dynamic_slice_in_dim(left, jnp.int32(0), le...]
    reduce_scatter x2, waiting for transfers between devices: 65 us -> 35.9 us  [row_sums(): lax.psum_scatter(contract(left, right, dims).astype(jnp.bfloat16), 'row',...]
    all_gather x2, waiting for transfers between devices: 110 us -> 127 us  [col_panel(): return lax.all_gather(values, 'col', axis=0, tiled=True)]
    ppermute x0 -> x6, starting transfers between devices: none -> 4.7 us  [gather_around(): held = lax.ppermute(held, axis, right)]
    unnamed x5 -> x13, local copies, waits for them, and re-layouts: 26.7 us -> 30.7 us
  transfers between devices with their start and end apart: 8 -> 12, of which waited for: 8 -> 9; matrix products, arithmetic and copies ran while one was open for 27% -> 26% of each run, Pallas kernels for 0% -> 0%
where the time goes in v1:
time: 412 us
  waiting for transfers between devices  265 us (64%)
  matrix products  91.9 us (22%)
  local copies, waits for them, and re-layouts  31.8 us (8%)
  between operations  14.3 us (3%)
  starting transfers between devices  4.93 us (1%)
    all_gather x2, waiting for transfers between devices, col_panel(): return lax.all_gather(values, 'col', axis=0, tiled=True)  127 us
    dot_general x6, matrix products, contract(): lax.dot_general(left, right, ((dims[0], dims[1]), ((), ())), preferred_el...  91.9 us
    ppermute x6, waiting for transfers between devices, gather_around(): held = lax.ppermute(held, axis, right)  59.6 us
    reduce_scatter x2, waiting for transfers between devices, col_sums(): lax.psum_scatter(contract(lax.dynamic_slice_in_dim(left, jnp.int32(0), le...  41.5 us
    reduce_scatter x2, waiting for transfers between devices, row_sums(): lax.psum_scatter(contract(left, right, dims).astype(jnp.bfloat16), 'row',...  35.9 us
    unnamed x13, local copies, waits for them, and re-layouts  30.7 us
  transfers between devices with their start and end apart: 12, of which 9 were waited for; matrix products, arithmetic and copies ran while one was open for 26% of the time, Pallas kernels for 0%

profile of v1, /device:TPU:0, one launch (start us, length us, event | category | flops | bytes accessed | tf_op | source)
XLA Modules:
  0.0 411.6 jit_solution(5870611346100683949)
XLA Ops:
  7.2 0.0 all-gather.3.cloned.1.call-start
  7.2 0.7 all-gather.3.cloned.1.call-update
  7.9 0.0 reduce-scatter.5.cloned.1.call-start
  7.9 65.4 %all-gather.3.cloned.1.call-done = bf16[512,3072]{1,0:T(8,128)(2,1)} async-done(((bf16[64,3072]{1,0:T(8,128)(2,1)}), bf16[512,3072]{1,0:T(8,128)(2,1)}) %all-gather.3.cloned.1.call-update) | async-done | bytes 3145744 | tf_op jit(solution)/shard_map/all_gather | solution.py:22
  73.4 15.9 %convolution_convert_fusion.4 = bf16[512,3072]{1,0:T(8,128)(2,1)} fusion(bf16[512,3072]{1,0:T(8,128)(2,1)} %all-gather.3.cloned.1.call-done, bf16[3072,3072]{1,0:T(8,128)(2,1)} %param.6), kind=kOutput, calls=%fused_computation.5 | convolution fusion | flops 9665249280 | bytes 25165824 | tf_op jit(solution)/shard_map/dot_general | solution.py:26
  89.2 0.0 reduce-scatter.5.cloned.1.call-update
  89.2 0.0 all-gather.5.cloned.1.call-start
  89.3 0.7 all-gather.5.cloned.1.call-update
  90.0 0.0 reduce-scatter.9.cloned.1.call-start
  90.0 35.9 %reduce-scatter.5.cloned.1.call-done = bf16[128,3072]{1,0:T(8,128)(2,1)} async-done(((bf16[512,3072]{1,0:T(8,128)(2,1)}), bf16[128,3072]{1,0:T(8,128)(2,1)}) %reduce-scatter.5.cloned.1.call-update) | async-done | bytes 786448 | tf_op jit(solution)/shard_map/reduce_scatter | solution.py:32
  126.0 1.7 fusion.8
  127.6 0.1 collective-permute-start
  127.7 61.2 %all-gather.5.cloned.1.call-done = bf16[512,3072]{1,0:T(8,128)(2,1)} async-done(((bf16[64,3072]{1,0:T(8,128)(2,1)}), bf16[512,3072]{1,0:T(8,128)(2,1)}) %all-gather.5.cloned.1.call-update) | async-done | bytes 3145744 | tf_op jit(solution)/shard_map/all_gather | solution.py:22
  188.9 15.9 %convolution_convert_fusion.2 = bf16[512,3072]{1,0:T(8,128)(2,1)} fusion(bf16[512,3072]{1,0:T(8,128)(2,1)} %all-gather.5.cloned.1.call-done, bf16[3072,3072]{1,0:T(8,128)(2,1)} %param.7), kind=kOutput, calls=%fused_computation.3 | convolution fusion | flops 9665249280 | bytes 25165824 | tf_op jit(solution)/shard_map/dot_general | solution.py:26
  204.7 0.0 reduce-scatter.9.cloned.1.call-update
  204.8 0.0 reduce-scatter.7.cloned.1.call-start
  204.8 0.1 collective-permute-start.1
  205.0 11.3 %collective-permute-done.1 = bf16[128,3072]{1,0:T(8,128)(2,1)S(1)} collective-permute-done((bf16[128,3072]{1,0:T(8,128)(2,1)S(1)}, bf16[128,3072]{1,0:T(8,128)(2,1)S(1)}, u32[]{:S(2)}, u32[]{:S(2)}) %collective-permute-start.1) | collective-permute-done | bytes 786464 | tf_op jit(solution)/shard_map/ppermute | solution.py:17
  216.3 0.4 broadcast.20.clone
  216.7 0.6 constant_dynamic-update-slice_fusion.7
  217.3 0.1 constant_dynamic-update-slice_fusion.6
  217.4 0.1 constant_dynamic-update-slice_fusion.5
  217.4 18.7 %collective-permute-done.2 = bf16[128,3072]{1,0:T(8,128)(2,1)S(1)} collective-permute-done((bf16[128,3072]{1,0:T(8,128)(2,1)S(1)}, bf16[128,3072]{1,0:T(8,128)(2,1)S(1)}, u32[]{:S(2)}, u32[]{:S(2)}) %collective-permute-start.2) | collective-permute-done | bytes 786464 | tf_op jit(solution)/shard_map/ppermute | solution.py:17
  236.2 0.1 constant_dynamic-update-slice_fusion.4
  236.3 1.6 copy-done.3
  237.9 15.0 %convolution_convert_fusion.3 = bf16[512,3072]{1,0:T(8,128)(2,1)} fusion(bf16[512,3072]{1,0:T(8,128)(2,1)S(1)} %constant_dynamic-update-slice_fusion.4, bf16[3072,3072]{1,0:T(8,128)(2,1)} %param.7), kind=kOutput, calls=%fused_computation.4 | convolution fusion | flops 9665249280 | bytes 25165824 | tf_op jit(solution)/shard_map/dot_general | solution.py:26
  252.9 0.0 reduce-scatter.7.cloned.1.call-update
  253.0 0.0 reduce-scatter.11.cloned.1.call-start
  253.0 0.0 reduce-scatter.9.cloned.1.call-done
  253.1 0.4 broadcast.20.clone.1
  253.4 0.7 copy-done.5
  254.2 1.2 constant_dynamic-update-slice_fusion.3
  255.4 1.6 collective-permute-start.3
  256.9 9.9 %collective-permute-done.3 = bf16[128,3072]{1,0:T(8,128)(2,1)S(1)} collective-permute-done((bf16[128,3072]{1,0:T(8,128)(2,1)S(1)}, bf16[128,3072]{1,0:T(8,128)(2,1)S(1)}, u32[]{:S(2)}, u32[]{:S(2)}) %collective-permute-start.3) | collective-permute-done | bytes 786464 | tf_op jit(solution)/shard_map/ppermute | solution.py:17
  266.8 1.5 collective-permute-start.4
  268.3 9.9 %collective-permute-done.4 = bf16[128,3072]{1,0:T(8,128)(2,1)S(1)} collective-permute-done((bf16[128,3072]{1,0:T(8,128)(2,1)S(1)}, bf16[128,3072]{1,0:T(8,128)(2,1)S(1)}, u32[]{:S(2)}, u32[]{:S(2)}) %collective-permute-start.4) | collective-permute-done | bytes 786464 | tf_op jit(solution)/shard_map/ppermute | solution.py:17
  278.3 1.5 collective-permute-start.5
  279.8 0.1 constant_dynamic-update-slice_fusion.2
  279.8 0.1 constant_dynamic-update-slice_fusion.1
  279.9 9.8 %collective-permute-done.5 = bf16[128,3072]{1,0:T(8,128)(2,1)S(1)} collective-permute-done((bf16[128,3072]{1,0:T(8,128)(2,1)S(1)}, bf16[128,3072]{1,0:T(8,128)(2,1)S(1)}, u32[]{:S(2)}, u32[]{:S(2)}) %collective-permute-start.5) | collective-permute-done | bytes 786464 | tf_op jit(solution)/shard_map/ppermute | solution.py:17
  289.7 0.1 constant_dynamic-update-slice_fusion
  289.8 1.7 copy-done.1
  291.4 15.0 %convolution_convert_fusion.1 = bf16[512,3072]{1,0:T(8,128)(2,1)} fusion(bf16[512,3072]{1,0:T(8,128)(2,1)S(1)} %constant_dynamic-update-slice_fusion, bf16[3072,3072]{1,0:T(8,128)(2,1)} %param.6), kind=kOutput, calls=%fused_computation.2 | convolution fusion | flops 9665249280 | bytes 25165824 | tf_op jit(solution)/shard_map/dot_general | solution.py:26
  306.5 1.9 copy-done.2
  308.4 15.0 %convert_bitcast_fusion = bf16[3072,3072]{0,1:T(8,128)(2,1)} fusion(bf16[512,3072]{1,0:T(8,128)(2,1)S(1)} %copy-done.2, bf16[512,3072]{1,0:T(8,128)(2,1)} %all-gather.3.cloned.1.call-done), kind=kOutput, calls=%fused_computation | convolution fusion | flops 9673113600 | bytes 25165824 | tf_op jit(solution)/shard_map/dot_general | solution.py:26
  323.4 24.8 %copy.8 = bf16[3072,3072]{1,0:T(8,128)(2,1)} copy(bf16[3072,3072]{0,1:T(8,128)(2,1)} %convert_bitcast_fusion) | data formatting | bytes 37748736
  348.2 15.1 %convolution_convert_fusion = bf16[3072,3072]{1,0:T(8,128)(2,1)} fusion(bf16[512,3072]{1,0:T(8,128)(2,1)S(1)} %copy-done.4, bf16[512,3072]{1,0:T(8,128)(2,1)} %all-gather.5.cloned.1.call-done), kind=kOutput, calls=%fused_computation.1 | convolution fusion | flops 9673113600 | bytes 25165824 | tf_op jit(solution)/shard_map/dot_general | solution.py:26
  363.2 41.5 %reduce-scatter.11.cloned.1.call-done = bf16[64,3072]{1,0:T(8,128)(2,1)} async-done(((bf16[512,3072]{1,0:T(8,128)(2,1)}), bf16[64,3072]{1,0:T(8,128)(2,1)}) %reduce-scatter.11.cloned.1.call-update) | async-done | bytes 393232 | tf_op jit(solution)/shard_map/reduce_scatter | solution.py:42
  (12 shorter events, 0.0 us)
Async XLA Ops:
  7.2 66.2 %all-gather.3.cloned.1.call-start = ((), (), s32[]{:S(2)}) async-start(), calls=%async_computation.4 | async-start | bytes 3538944 | tf_op jit(solution)/shard_map/all_gather | solution.py:22
  7.9 118.1 %reduce-scatter.5.cloned.1.call-start = ((), (), s32[]{:S(2)}) async-start(), calls=%async_computation.5 | async-start | bytes 3932160 | tf_op jit(solution)/shard_map/reduce_scatter | solution.py:32
  89.2 99.6 %all-gather.5.cloned.1.call-start = ((), (), s32[]{:S(2)}) async-start(), calls=%async_computation.7 | async-start | bytes 3538944 | tf_op jit(solution)/shard_map/all_gather | solution.py:22
  90.0 163.1 %reduce-scatter.9.cloned.1.call-start = ((), (), s32[]{:S(2)}) async-start(), calls=%async_computation.8 | async-start | bytes 3932160 | tf_op jit(solution)/shard_map/reduce_scatter | solution.py:32
  127.6 77.2 %collective-permute-start = (bf16[128,3072]{1,0:T(8,128)(2,1)S(1)}, bf16[128,3072]{1,0:T(8,128)(2,1)S(1)}, u32[]{:S(2)}, u32[]{:S(2)}) collective-permute-start(bf16[128,3072]{1,0:T(8,128)(2,1)S(1)} %fusion.8), channel_id=1, source_target_pairs={{0,8},{8,16},{16,24},{24,0},{1,9},{9,17},{17,25},{25,1},{2,10},{10... | collective-permute-start | bytes 2359304 | tf_op jit(solution)/shard_map/ppermute | solution.py:17
  204.7 11.9 %copy-start = (bf16[128,3072]{1,0:T(8,128)(2,1)S(1)}, bf16[128,3072]{1,0:T(8,128)(2,1)}, u32[]{:S(2)}) copy-start(bf16[128,3072]{1,0:T(8,128)(2,1)} %reduce-scatter.5.cloned.1.call-done) | copy-start | bytes 2359300
  204.8 158.5 %reduce-scatter.7.cloned.1.call-start = ((), (), s32[]{:S(2)}) async-start(), calls=%async_computation.6 | async-start | bytes 3538944 | tf_op jit(solution)/shard_map/reduce_scatter | solution.py:42
  204.8 11.5 %collective-permute-start.1 = (bf16[128,3072]{1,0:T(8,128)(2,1)S(1)}, bf16[128,3072]{1,0:T(8,128)(2,1)S(1)}, u32[]{:S(2)}, u32[]{:S(2)}) collective-permute-start(bf16[128,3072]{1,0:T(8,128)(2,1)S(1)} %collective-permute-done), channel_id=1, source_target_pairs={{0,8},{8,16},{16,24},{24,0},{1,9},{9,17},{17,25},{25,1},{2,10},{10... | collective-permute-start | bytes 2359304 | tf_op jit(solution)/shard_map/ppermute | solution.py:17
  216.3 19.9 %collective-permute-start.2 = (bf16[128,3072]{1,0:T(8,128)(2,1)S(1)}, bf16[128,3072]{1,0:T(8,128)(2,1)S(1)}, u32[]{:S(2)}, u32[]{:S(2)}) collective-permute-start(bf16[128,3072]{1,0:T(8,128)(2,1)S(1)} %collective-permute-done.1), channel_id=1, source_target_pairs={{0,8},{8,16},{16,24},{24,0},{1,9},{9,17},{17,25},{25,1},{2,10},{10... | collective-permute-start | bytes 2359304 | tf_op jit(solution)/shard_map/ppermute | solution.py:17
  236.3 1.6 copy-start.3
  253.0 151.7 %reduce-scatter.11.cloned.1.call-start = ((), (), s32[]{:S(2)}) async-start(), calls=%async_computation.9 | async-start | bytes 3538944 | tf_op jit(solution)/shard_map/reduce_scatter | solution.py:42
  253.0 1.1 copy-start.5
  255.4 11.5 %collective-permute-start.3 = (bf16[128,3072]{1,0:T(8,128)(2,1)S(1)}, bf16[128,3072]{1,0:T(8,128)(2,1)S(1)}, u32[]{:S(2)}, u32[]{:S(2)}) collective-permute-start(bf16[128,3072]{1,0:T(8,128)(2,1)S(1)} %get-tuple-element.9), channel_id=1, source_target_pairs={{0,8},{8,16},{16,24},{24,0},{1,9},{9,17},{17,25},{25,1},{2,10},{10... | collective-permute-start | bytes 2359304 | tf_op jit(solution)/shard_map/ppermute | solution.py:17
  266.8 11.4 %collective-permute-start.4 = (bf16[128,3072]{1,0:T(8,128)(2,1)S(1)}, bf16[128,3072]{1,0:T(8,128)(2,1)S(1)}, u32[]{:S(2)}, u32[]{:S(2)}) collective-permute-start(bf16[128,3072]{1,0:T(8,128)(2,1)S(1)} %collective-permute-done.3), channel_id=1, source_target_pairs={{0,8},{8,16},{16,24},{24,0},{1,9},{9,17},{17,25},{25,1},{2,10},{10... | collective-permute-start | bytes 2359304 | tf_op jit(solution)/shard_map/ppermute | solution.py:17
  278.3 11.4 %collective-permute-start.5 = (bf16[128,3072]{1,0:T(8,128)(2,1)S(1)}, bf16[128,3072]{1,0:T(8,128)(2,1)S(1)}, u32[]{:S(2)}, u32[]{:S(2)}) collective-permute-start(bf16[128,3072]{1,0:T(8,128)(2,1)S(1)} %collective-permute-done.4), channel_id=1, source_target_pairs={{0,8},{8,16},{16,24},{24,0},{1,9},{9,17},{17,25},{25,1},{2,10},{10... | collective-permute-start | bytes 2359304 | tf_op jit(solution)/shard_map/ppermute | solution.py:17
  289.7 1.7 copy-start.1
  306.5 1.9 copy-start.2
  323.4 24.8 %copy-start.4 = (bf16[512,3072]{1,0:T(8,128)(2,1)S(1)}, bf16[512,3072]{1,0:T(8,128)(2,1)}, u32[]{:S(2)}) copy-start(bf16[512,3072]{1,0:T(8,128)(2,1)} %copy-done.3) | copy-start | bytes 9437188
Sparse Core Ops, SparseCore 0:
  10.2 63.1 all-gather.2
  89.4 36.5 reduce-scatter.4
  128.4 60.4 all-gather.4
  204.9 40.9 reduce-scatter.8
  253.1 74.2 reduce-scatter.6
  331.4 73.3 reduce-scatter.10
